TPU v7x, 512 devices: a whole 4x8x8 slice. The times are simulated.
512 devices in a mesh: snode: 64 (over z, y), rows: 8 (over x, core).
Axes of the slice: x: 4, y: 8, z: 8, core: 2. Of those that a mesh axis runs over, the one named last changes fastest.
Arguments:
- anc_store: bfloat16 [8192, 8192], P('snode'), may hold values from -9 to 9
- patterns: int32 [64, 8], replicated, may hold values from 0 to 63, all different within a row
- tile_counts: int32 [64], replicated, may hold values from 1 to 8, 448 in all
- tile_owner: int32 [64], replicated, may hold values from 0 to 63, as said below
- l_offdiag: bfloat16 [65536, 512], P(('snode', 'rows')), may hold values from -0.25 to 0.25
- diag_inverse: bfloat16 [32768, 512], P(('snode', 'rows')), may hold values from -1 to 2, as said below
Outputs:
- sigma_offdiag: bfloat16 [65536, 512], P(('snode', 'rows'))
- sigma_diag: float32 [32768, 512], P(('snode', 'rows'))
Inputs may be any that keep to these rules, and one draw needn't show every extreme that they name: `patterns`: each supernode's row names 8 different ancestor tiles. Slots before tile_counts[s] of a supernode's pattern are live, the rest padding; some supernode has all 8 slots live. `tile_owner`: a permutation of the ancestor tiles. `diag_inverse`: each supernode's block of 512 rows is lower triangular with diagonal entries between 1 and 2.
All inputs are finite; a program needn't handle non-finite values.
Results may differ from a plain program's by a relative error of at most 0.014.
Values may be sent and summed in bfloat16 or wider, within the bound.
A program may use at most 64 MiB of HBM per device.

v0:
```python
import jax
import jax.numpy as jnp
from jax import lax
from jax.sharding import PartitionSpec as P


def row_block(matrix, index):
    return lax.dynamic_index_in_dim(matrix, index, 0, keepdims=False)


def per_device(anc_store, patterns, tile_counts, tile_owner, l_offdiag, diag_inverse):
    tile_rows = anc_store.shape[0]
    pool_size = tile_owner.shape[0]
    group_count = patterns.shape[0]
    pattern_len = patterns.shape[1]
    group_id = lax.axis_index("snode")
    part_id = lax.axis_index("rows")
    local_tiles = l_offdiag.shape[0] // tile_rows
    band_rows = diag_inverse.shape[0]
    band_start = part_id * band_rows
    live_mask = jnp.arange(pattern_len, dtype=jnp.int32)[None, :] < tile_counts[:, None]
    own_live = lax.dynamic_slice_in_dim(
        row_block(live_mask, group_id), part_id * local_tiles, local_tiles
    )
    keep_rows = jnp.repeat(own_live, tile_rows)
    masked_l = jnp.where(keep_rows[:, None], l_offdiag, jnp.zeros_like(l_offdiag))
    piece = lax.all_gather(diag_inverse, "rows", axis=0, tiled=True)
    u_total = jnp.dot(masked_l, piece, preferred_element_type=jnp.float32)
    own_cols = lax.dynamic_slice_in_dim(piece, band_start, band_rows, 1)
    d_total = lax.dot_general(
        own_cols, piece, (((0,), (0,)), ((), ())), preferred_element_type=jnp.float32
    )
    u_total, base_diag = (u_total, d_total)
    u_factor = u_total.astype(jnp.bfloat16)
    owned_tile = jnp.sum(
        jnp.arange(pool_size, dtype=jnp.int32) * (tile_owner == group_id).astype(jnp.int32)
    )
    send_flag = jnp.any((patterns == owned_tile) & live_mask, axis=1)
    own_pattern = row_block(patterns, group_id)
    sources = jnp.take(tile_owner, own_pattern, axis=0)
    col_tiles = lax.dynamic_slice_in_dim(patterns, part_id * local_tiles, local_tiles, 1)
    stored_blocks = anc_store.reshape(tile_rows, pool_size, tile_rows)
    picked = jnp.take(stored_blocks, col_tiles, axis=1)
    picked = jnp.transpose(picked, (1, 0, 2, 3)).reshape(
        group_count, tile_rows, local_tiles * tile_rows
    )
    outgoing = jnp.where(send_flag[:, None, None], picked, jnp.zeros_like(picked))
    incoming = lax.all_to_all(outgoing, "snode", split_axis=0, concat_axis=0, tiled=True)
    arranged = jnp.take(incoming, sources, axis=0).reshape(
        pattern_len * tile_rows, local_tiles * tile_rows
    )
    own_rows = lax.all_to_all(arranged, "rows", split_axis=0, concat_axis=1, tiled=True)
    y_block = jnp.dot(
        own_rows,
        lax.all_gather(u_factor, "rows", axis=0, tiled=True),
        preferred_element_type=jnp.float32,
    )
    offdiag = (-y_block).astype(jnp.bfloat16)
    partial_diag = lax.dot_general(
        u_factor, offdiag, (((0,), (0,)), ((), ())), preferred_element_type=jnp.float32
    )
    whole_update = lax.psum(partial_diag.astype(jnp.bfloat16), "rows").astype(jnp.float32)
    reduced = lax.dynamic_slice_in_dim(whole_update, band_start, band_rows, 0)
    return (offdiag, base_diag - reduced)


def solution(mesh):
    in_specs = (
        P("snode", None),
        P(),
        P(),
        P(),
        P(("snode", "rows"), None),
        P(("snode", "rows"), None),
    )
    out_specs = (P(("snode", "rows"), None), P(("snode", "rows"), None))
    return jax.shard_map(
        per_device, mesh=mesh, in_specs=in_specs, out_specs=out_specs, check_vma=False
    )
```

profile of v0, /device:TPU:8, one launch (start us, length us, event | category | flops | bytes accessed | tf_op | source)
XLA Modules:
  0.0 179.3 jit_solution(5158815995826037886)
XLA Ops:
  7.2 0.7 and_bitcast_fusion
  7.9 3.2 %copy.8 = bf16[128,8192]{0,1:T(8,128)(2,1)S(1)} copy(bf16[128,8192]{1,0:T(8,128)(2,1)} %param.6) | data formatting | bytes 4194304 | tf_op args[0]
  11.1 2.9 %copy.9 = bf16[128,64,128]{2,0,1:T(8,128)(2,1)} copy(bf16[128,64,128]{0,2,1:T(8,128)(2,1)S(1)} %bitcast.37) | data formatting | bytes 4194304 | tf_op jit(solution)/shard_map/reshape | solution.py:42
  14.0 2.6 %gather_fusion.1 = bf16[64,128,128]{2,1,0:T(8,128)(2,1)S(1)} fusion(bf16[128,64,128]{2,0,1:T(8,128)(2,1)} %copy.9, s32[1024]{0:T(1024)S(1)} %pad_clamp_fusion.1), kind=kCustom, calls=%fused_computation.1 | custom fusion | bytes 4194560 | tf_op jit(solution)/shard_map/jit(_take)/gather | solution.py:43
  16.6 0.6 fusion.6
  17.3 0.7 iota_compare_fusion
  17.9 1.7 bitcast_select_fusion
  19.6 16.7 %all-to-all-start = ((bf16[64,128,128]{2,1,0:T(8,128)(2,1)}), bf16[64,128,128]{2,1,0:T(8,128)(2,1)S(1)}, u32[]{:S(2)}, u32[]{:S(2)}) async-start(bf16[64,128,128]{2,1,0:T(8,128)(2,1)} %bitcast_select_fusion), calls=%async_computation | async-start | bytes 4194304 | tf_op jit(solution)/shard_map/all_to_all | solution.py:48
  36.3 0.0 all-gather.2.cloned.1.call-start
  36.4 0.6 dynamic_slice.22
  37.0 13.4 %all_gather.6 = bf16[512,512]{1,0:T(8,128)(2,1)S(1)} all-gather(bf16[64,512]{1,0:T(8,128)(2,1)S(1)} %copy-done.4), channel_id=1, replica_groups=mesh['snode'=64,'rows'=8] {'rows'}, dimensions={0}, use_global_device_ids=true | all-gather | bytes 589824 | tf_op jit(solution)/shard_map/all_gather | solution.py:27
  50.4 1.5 convolution_convert_fusion.1
  52.0 0.0 all-reduce.2.cloned.1.call-start
  52.0 0.2 dynamic-slice_reduce_fusion
  52.2 0.6 gather_fusion
  52.9 36.3 %all-to-all-done = bf16[64,128,128]{2,1,0:T(8,128)(2,1)S(1)} async-done(((bf16[64,128,128]{2,1,0:T(8,128)(2,1)}), bf16[64,128,128]{2,1,0:T(8,128)(2,1)S(1)}, u32[]{:S(2)}, u32[]{:S(2)}) %all-to-all-start) | async-done | bytes 2097184 | tf_op jit(solution)/shard_map/all_to_all | solution.py:48
  89.2 0.6 gather_fusion.2
  89.8 0.1 broadcast_select_fusion
  89.9 11.6 %all_to_all.21 = bf16[8,128,128]{2,1,0:T(8,128)(2,1)S(1)} all-to-all(bf16[8,128,128]{2,1,0:T(8,128)(2,1)S(1)} %broadcast_select_fusion), channel_id=1, replica_groups=mesh['snode'=64,'rows'=8] {'rows'}, dimensions={0} | all-to-all | bytes 524288 | tf_op jit(solution)/shard_map/all_to_all | solution.py:52
  101.6 0.2 copy.10
  101.8 1.6 fusion
  103.4 1.1 convolution_convert_fusion
  104.5 66.2 %all-reduce.2.cloned.1.call-done = bf16[512,512]{1,0:T(8,128)(2,1)} async-done(((bf16[512,512]{1,0:T(8,128)(2,1)}), bf16[512,512]{1,0:T(8,128)(2,1)}) %all-reduce.2.cloned.1.call-update) | async-done | bytes 524304 | tf_op jit(solution)/shard_map/psum | solution.py:62
  170.7 1.8 %convolution_subtract_fusion = f32[64,512]{1,0:T(8,128)} fusion(bf16[512,512]{1,0:T(8,128)(2,1)S(1)} %all_gather.6, s32[]{:T(128)S(6)} %select_n.116, bf16[512,512]{1,0:T(8,128)(2,1)} %all-reduce.2.cloned.1.call-done), kind=kOutput, calls=%fused_computation.9 | convolution fusion | flops 33619968 | bytes 852992 | tf_op jit(solution)/shard_map/dot_general | solution.py:30
  (23 shorter events, 0.1 us)
Async XLA Ops:
  14.0 2.6 %copy-start = (s32[64]{0:T(128)S(1)}, s32[64]{0:T(128)}, u32[]{:S(2)}) copy-start(s32[64]{0:T(128)} %param.9) | copy-start | bytes 772
  14.0 3.2 %copy-start.5 = (s32[64,8]{0,1:T(8,128)S(1)}, s32[64,8]{0,1:T(8,128)}, u32[]{:S(2)}) copy-start(s32[64,8]{0,1:T(8,128)} %param.7) | copy-start | bytes 6148
  14.0 3.2 %copy-start.6 = (s32[64]{0:T(128)S(1)}, s32[64]{0:T(128)}, u32[]{:S(2)}) copy-start(s32[64]{0:T(128)} %param.8) | copy-start | bytes 772
  19.6 17.4 %copy-start.4 = (bf16[64,512]{1,0:T(8,128)(2,1)S(1)}, bf16[64,512]{1,0:T(8,128)(2,1)}, u32[]{:S(2)}) copy-start(bf16[64,512]{1,0:T(8,128)(2,1)} %param.11) | copy-start | bytes 196612
  19.6 30.8 %copy-start.3 = (bf16[128,512]{1,0:T(8,128)(2,1)S(1)}, bf16[128,512]{1,0:T(8,128)(2,1)}, u32[]{:S(2)}) copy-start(bf16[128,512]{1,0:T(8,128)(2,1)} %param.10) | copy-start | bytes 393220
  19.6 69.6 %all-to-all-start = ((bf16[64,128,128]{2,1,0:T(8,128)(2,1)}), bf16[64,128,128]{2,1,0:T(8,128)(2,1)S(1)}, u32[]{:S(2)}, u32[]{:S(2)}) async-start(bf16[64,128,128]{2,1,0:T(8,128)(2,1)} %bitcast_select_fusion), calls=%async_computation | async-start | bytes 4194304 | tf_op jit(solution)/shard_map/all_to_all | solution.py:48
  36.3 65.5 %all-gather.2.cloned.1.call-start = ((), (), s32[]{:S(2)}) async-start(), calls=%async_computation.2 | async-start | bytes 1179648 | tf_op jit(solution)/shard_map/all_gather | solution.py:55
  52.0 51.4 %copy-start.1 = (bf16[128,512]{1,0:T(8,128)(2,1)S(1)}, bf16[128,512]{1,0:T(8,128)(2,1)}, u32[]{:S(2)}) copy-start(bf16[128,512]{1,0:T(8,128)(2,1)} %convolution_convert_fusion.1) | copy-start | bytes 393220
  52.0 118.7 %all-reduce.2.cloned.1.call-start = ((), (), s32[]{:S(2)}) async-start(), calls=%async_computation.3 | async-start | bytes 1048576 | tf_op jit(solution)/shard_map/psum | solution.py:62
  103.4 69.1 %copy-start.2 = (bf16[128,512]{1,0:T(8,128)(2,1)}, bf16[128,512]{1,0:T(8,128)(2,1)S(1)}, u32[]{:S(2)}) copy-start(bf16[128,512]{1,0:T(8,128)(2,1)S(1)} %fusion) | copy-start | bytes 393220
Sparse Core Ops, SparseCore 0:
  52.1 28.7 all-gather.1
  104.6 65.9 all-reduce.1
where the time goes:
time: 180 us; the launch traced here: 179 us
  waiting for transfers between devices  103 us (57%)
  blocking collectives  25.1 us (14%)
  starting transfers between devices  16.8 us (9%)
  between operations  14.2 us (8%)
  local copies, waits for them, and re-layouts  10.9 us (6%)
  matrix products  6 us (3%)
  other arithmetic  3.82 us (2%)
    psum x1, waiting for transfers between devices, per_device(): lax.psum(partial_diag.astype(jnp.bfloat16), 'rows').astype(jnp.float32)  66.2 us
    all_to_all x1, waiting for transfers between devices, per_device(): lax.all_to_all(outgoing, 'snode', split_axis=0, concat_axis=0, tiled=True)  36.3 us
    all_to_all x1, starting transfers between devices, per_device(): lax.all_to_all(outgoing, 'snode', split_axis=0, concat_axis=0, tiled=True)  16.7 us
    all_gather x1, blocking collectives, per_device(): piece = lax.all_gather(diag_inverse, 'rows', axis=0, tiled=True)  13.4 us
    all_to_all x1, blocking collectives, per_device(): lax.all_to_all(arranged, 'rows', split_axis=0, concat_axis=1, tiled=True)  11.6 us
  transfers between devices with their start and end apart: 3, of which 2 were waited for; matrix products, arithmetic and copies ran while one was open for 2% of the time, Pallas kernels for 0%

commit v1 on v0

--- a/solution.py
+++ b/solution.py
@@ -24,7 +24,9 @@
     )
     keep_rows = jnp.repeat(own_live, tile_rows)
     masked_l = jnp.where(keep_rows[:, None], l_offdiag, jnp.zeros_like(l_offdiag))
-    piece = lax.all_gather(diag_inverse, "rows", axis=0, tiled=True)
+    piece = jnp.concatenate(
+        lax.all_to_all(jnp.stack([diag_inverse] * lax.axis_size("rows")), "rows", 0, 0), axis=0
+    )
     u_total = jnp.dot(masked_l, piece, preferred_element_type=jnp.float32)
     own_cols = lax.dynamic_slice_in_dim(piece, band_start, band_rows, 1)
     d_total = lax.dot_general(

time: 180 us -> 188 us (1.044)
  waiting for transfers between devices: 103 us -> 118 us
  blocking collectives: 25.1 us -> 11.3 us
  starting transfers between devices: 16.8 us -> 21.1 us
    all_to_all x1, waiting for transfers between devices: 36.3 us -> 50.3 us  [per_device(): lax.all_to_all(outgoing, 'snode', split_axis=0, concat_axis=0, tiled=True)]
    all_gather x1 -> x0, blocking collectives: 13.4 us -> none  [per_device(): piece = lax.all_gather(diag_inverse, 'rows', axis=0, tiled=True)]
    all_to_all x0 -> x1, starting transfers between devices: none -> 4.3 us  [per_device(): lax.all_to_all(jnp.stack([diag_inverse] * lax.axis_size('rows')), 'rows',...]
  transfers between devices with their start and end apart: 3 -> 4, of which waited for: 2 -> 2; matrix products, arithmetic and copies ran while one was open for 2% -> 9% of each run, Pallas kernels for 0% -> 0%
where the time goes in v1:
time: 188 us; the launch traced here: 187 us
  waiting for transfers between devices  118 us (63%)
  starting transfers between devices  21.1 us (11%)
  between operations  14.2 us (8%)
  local copies, waits for them, and re-layouts  12.6 us (7%)
  blocking collectives  11.3 us (6%)
  matrix products  6.01 us (3%)
  other arithmetic  3.82 us (2%)
    psum x1, waiting for transfers between devices, per_device(): lax.psum(partial_diag.astype(jnp.bfloat16), 'rows').astype(jnp.float32)  68 us
    all_to_all x1, waiting for transfers between devices, per_device(): lax.all_to_all(outgoing, 'snode', split_axis=0, concat_axis=0, tiled=True)  50.3 us
    all_to_all x1, starting transfers between devices, per_device(): lax.all_to_all(outgoing, 'snode', split_axis=0, concat_axis=0, tiled=True)  16.7 us
    all_to_all x1, blocking collectives, per_device(): lax.all_to_all(arranged, 'rows', split_axis=0, concat_axis=1, tiled=True)  11.3 us
    all_to_all x1, starting transfers between devices, per_device(): lax.all_to_all(jnp.stack([diag_inverse] * lax.axis_size('rows')), 'rows',...  4.3 us
  transfers between devices with their start and end apart: 4, of which 2 were waited for; matrix products, arithmetic and copies ran while one was open for 9% of the time, Pallas kernels for 0%

profile of v1, /device:TPU:8, one launch (start us, length us, event | category | flops | bytes accessed | tf_op | source)
XLA Modules:
  0.0 187.5 jit_solution(7721786729033643407)
XLA Ops:
  7.2 1.7 stack.2
  8.8 4.3 %all-to-all-start.2 = ((bf16[8,64,512]{2,1,0:T(8,128)(2,1)}), bf16[8,64,512]{2,1,0:T(8,128)(2,1)S(1)}, u32[]{:S(2)}, u32[]{:S(2)}) async-start(bf16[8,64,512]{2,1,0:T(8,128)(2,1)} %stack.2), calls=%async_computation.2 | async-start | bytes 1048576 | tf_op jit(solution)/shard_map/all_to_all | solution.py:28
  13.2 0.7 and_bitcast_fusion
  13.9 3.2 %copy.8 = bf16[128,8192]{0,1:T(8,128)(2,1)S(1)} copy(bf16[128,8192]{1,0:T(8,128)(2,1)} %param.6) | data formatting | bytes 4194304 | tf_op args[0]
  17.1 2.9 %copy.9 = bf16[128,64,128]{2,0,1:T(8,128)(2,1)} copy(bf16[128,64,128]{0,2,1:T(8,128)(2,1)S(1)} %bitcast.38) | data formatting | bytes 4194304 | tf_op jit(solution)/shard_map/reshape | solution.py:44
  20.0 2.6 %gather_fusion.1 = bf16[64,128,128]{2,1,0:T(8,128)(2,1)S(1)} fusion(bf16[128,64,128]{2,0,1:T(8,128)(2,1)} %copy.9, s32[1024]{0:T(1024)S(1)} %pad_clamp_fusion.1), kind=kCustom, calls=%fused_computation.1 | custom fusion | bytes 4194560 | tf_op jit(solution)/shard_map/jit(_take)/gather | solution.py:45
  22.6 0.6 fusion.6
  23.3 0.7 iota_compare_fusion
  23.9 1.7 bitcast_select_fusion
  25.6 16.7 %all-to-all-start = ((bf16[64,128,128]{2,1,0:T(8,128)(2,1)}), bf16[64,128,128]{2,1,0:T(8,128)(2,1)S(1)}, u32[]{:S(2)}, u32[]{:S(2)}) async-start(bf16[64,128,128]{2,1,0:T(8,128)(2,1)} %bitcast_select_fusion), calls=%async_computation | async-start | bytes 4194304 | tf_op jit(solution)/shard_map/all_to_all | solution.py:50
  42.4 0.6 dynamic_slice.22
  43.0 1.5 convolution_convert_fusion.1
  44.6 0.0 all-reduce.2.cloned.1.call-start
  44.6 0.2 dynamic-slice_reduce_fusion
  44.8 0.6 gather_fusion
  45.5 50.3 %all-to-all-done = bf16[64,128,128]{2,1,0:T(8,128)(2,1)S(1)} async-done(((bf16[64,128,128]{2,1,0:T(8,128)(2,1)}), bf16[64,128,128]{2,1,0:T(8,128)(2,1)S(1)}, u32[]{:S(2)}, u32[]{:S(2)}) %all-to-all-start) | async-done | bytes 2097184 | tf_op jit(solution)/shard_map/all_to_all | solution.py:50
  95.8 0.6 gather_fusion.2
  96.4 0.1 broadcast_select_fusion
  96.5 11.3 %all_to_all.26 = bf16[8,128,128]{2,1,0:T(8,128)(2,1)S(1)} all-to-all(bf16[8,128,128]{2,1,0:T(8,128)(2,1)S(1)} %broadcast_select_fusion), channel_id=1, replica_groups=mesh['snode'=64,'rows'=8] {'rows'}, dimensions={0} | all-to-all | bytes 524288 | tf_op jit(solution)/shard_map/all_to_all | solution.py:54
  107.9 0.2 copy.10
  108.1 1.6 fusion
  109.7 1.1 convolution_convert_fusion
  110.8 68.0 %all-reduce.2.cloned.1.call-done = bf16[512,512]{1,0:T(8,128)(2,1)} async-done(((bf16[512,512]{1,0:T(8,128)(2,1)}), bf16[512,512]{1,0:T(8,128)(2,1)}) %all-reduce.2.cloned.1.call-update) | async-done | bytes 524304 | tf_op jit(solution)/shard_map/psum | solution.py:64
  178.8 1.8 convolution_subtract_fusion
  (23 shorter events, 0.2 us)
Async XLA Ops:
  8.8 16.8 %all-to-all-start.2 = ((bf16[8,64,512]{2,1,0:T(8,128)(2,1)}), bf16[8,64,512]{2,1,0:T(8,128)(2,1)S(1)}, u32[]{:S(2)}, u32[]{:S(2)}) async-start(bf16[8,64,512]{2,1,0:T(8,128)(2,1)} %stack.2), calls=%async_computation.2 | async-start | bytes 1048576 | tf_op jit(solution)/shard_map/all_to_all | solution.py:28
  20.0 2.6 %copy-start = (s32[64]{0:T(128)S(1)}, s32[64]{0:T(128)}, u32[]{:S(2)}) copy-start(s32[64]{0:T(128)} %param.9) | copy-start | bytes 772
  20.0 3.2 %copy-start.4 = (s32[64,8]{0,1:T(8,128)S(1)}, s32[64,8]{0,1:T(8,128)}, u32[]{:S(2)}) copy-start(s32[64,8]{0,1:T(8,128)} %param.7) | copy-start | bytes 6148
  20.0 3.2 %copy-start.5 = (s32[64]{0:T(128)S(1)}, s32[64]{0:T(128)}, u32[]{:S(2)}) copy-start(s32[64]{0:T(128)} %param.8) | copy-start | bytes 772
  25.6 17.4 %copy-start.3 = (bf16[128,512]{1,0:T(8,128)(2,1)S(1)}, bf16[128,512]{1,0:T(8,128)(2,1)}, u32[]{:S(2)}) copy-start(bf16[128,512]{1,0:T(8,128)(2,1)} %param.10) | copy-start | bytes 393220
  25.6 70.2 %all-to-all-start = ((bf16[64,128,128]{2,1,0:T(8,128)(2,1)}), bf16[64,128,128]{2,1,0:T(8,128)(2,1)S(1)}, u32[]{:S(2)}, u32[]{:S(2)}) async-start(bf16[64,128,128]{2,1,0:T(8,128)(2,1)} %bitcast_select_fusion), calls=%async_computation | async-start | bytes 4194304 | tf_op jit(solution)/shard_map/all_to_all | solution.py:50
  42.3 65.7 %all-gather.2.cloned.1.call-start = ((), (), s32[]{:S(2)}) async-start(), calls=%async_computation.3 | async-start | bytes 1179648 | tf_op jit(solution)/shard_map/all_gather | solution.py:57
  44.5 65.1 %copy-start.1 = (bf16[128,512]{1,0:T(8,128)(2,1)S(1)}, bf16[128,512]{1,0:T(8,128)(2,1)}, u32[]{:S(2)}) copy-start(bf16[128,512]{1,0:T(8,128)(2,1)} %convolution_convert_fusion.1) | copy-start | bytes 393220
  44.6 134.3 %all-reduce.2.cloned.1.call-start = ((), (), s32[]{:S(2)}) async-start(), calls=%async_computation.4 | async-start | bytes 1048576 | tf_op jit(solution)/shard_map/psum | solution.py:64
  109.7 71.0 %copy-start.2 = (bf16[128,512]{1,0:T(8,128)(2,1)}, bf16[128,512]{1,0:T(8,128)(2,1)S(1)}, u32[]{:S(2)}) copy-start(bf16[128,512]{1,0:T(8,128)(2,1)S(1)} %fusion) | copy-start | bytes 393220
Sparse Core Ops, SparseCore 0:
  45.9 29.8 all-gather.1
  110.9 67.8 all-reduce.1
